TPU v7x, 32 devices: a whole 2x2x4 slice. The times are simulated.
32 devices in a mesh: wide: 16 (over z, y, x), narrow: 2 (over core).
Axes of the slice: x: 2, y: 2, z: 4, core: 2. Of those that a mesh axis runs over, the one named last changes fastest.
Arguments:
- activations: bfloat16 [16384, 1024], P(('wide', 'narrow')), may hold values from -6 to 6
- segment_ids: int32 [16384], P(('wide', 'narrow')), may hold values from -1 to 511, as said below
- cotangent: bfloat16 [16384, 1024], P(('wide', 'narrow')), may hold values from -6 to 6
- querymat: bfloat16 [1024, 1024], P(('wide', 'narrow')), may hold values from -0.1875 to 0.1875
- keymat: bfloat16 [1024, 1024], P(('wide', 'narrow')), may hold values from -0.1875 to 0.1875
- valuemat: bfloat16 [1024, 1024], P(('wide', 'narrow')), may hold values from -0.1875 to 0.1875
- outmat: bfloat16 [1024, 1024], P(('wide', 'narrow')), may hold values from -0.1875 to 0.1875
- upmatrix: bfloat16 [1024, 4096], P(('wide', 'narrow')), may hold values from -0.1875 to 0.1875
- downmatrix: bfloat16 [4096, 1024], P(('wide', 'narrow')), may hold values from -0.09375 to 0.09375
- querybias: bfloat16 [1024], P(('wide', 'narrow')), may hold values from -3 to 3
- keybias: bfloat16 [1024], P(('wide', 'narrow')), may hold values from -3 to 3
- valuebias: bfloat16 [1024], P(('wide', 'narrow')), may hold values from -3 to 3
- outbias: bfloat16 [1024], P(('wide', 'narrow')), may hold values from -3 to 3
- upbias: bfloat16 [4096], P(('wide', 'narrow')), may hold values from -3 to 3
- downbias: bfloat16 [1024], P(('wide', 'narrow')), may hold values from -3 to 3
- firstgain: bfloat16 [1024], P(('wide', 'narrow')), may hold values from 0.099609375 to 1.8984375
- secondgain: bfloat16 [1024], P(('wide', 'narrow')), may hold values from 0.099609375 to 1.8984375
- thirdgain: bfloat16 [1024], P(('wide', 'narrow')), may hold values from 0.099609375 to 1.8984375
- fourthgain: bfloat16 [1024], P(('wide', 'narrow')), may hold values from 0.099609375 to 1.8984375
Outputs:
- layer_out: bfloat16 [16384, 1024], P(('wide', 'narrow'))
- input_gradient: float32 [16384, 1024], P(('wide', 'narrow'))
- querymat_gradient: float32 [1024, 1024], P(('wide', 'narrow'))
- keymat_gradient: float32 [1024, 1024], P(('wide', 'narrow'))
- valuemat_gradient: float32 [1024, 1024], P(('wide', 'narrow'))
- outmat_gradient: float32 [1024, 1024], P(('wide', 'narrow'))
- upmatrix_gradient: float32 [1024, 4096], P(('wide', 'narrow'))
- downmatrix_gradient: float32 [4096, 1024], P(('wide', 'narrow'))
- querybias_gradient: float32 [1024], P(('wide', 'narrow'))
- keybias_gradient: float32 [1024], P(('wide', 'narrow'))
- valuebias_gradient: float32 [1024], P(('wide', 'narrow'))
- outbias_gradient: float32 [1024], P(('wide', 'narrow'))
- upbias_gradient: float32 [4096], P(('wide', 'narrow'))
- downbias_gradient: float32 [1024], P(('wide', 'narrow'))
- firstgain_gradient: float32 [1024], P(('wide', 'narrow'))
- secondgain_gradient: float32 [1024], P(('wide', 'narrow'))
- thirdgain_gradient: float32 [1024], P(('wide', 'narrow'))
- fourthgain_gradient: float32 [1024], P(('wide', 'narrow'))
- output_power: float32 [], replicated
Inputs may be any that keep to these rules, and one draw needn't show every extreme that they name: `segment_ids`: in each packed row of 512 slots the ids of the used slots start at 0 and never fall, each sequence being a run of equal ids; the used slots come first, 128 or more of them, and the rest hold -1; some row holds one sequence of 512 tokens, and some row holds 512 sequences of one token.
All inputs are finite; a program needn't handle non-finite values.
Results may differ from a plain program's by a relative error of at most 0.019.
Values may be sent and summed in bfloat16 or wider, within the bound.
No kernel may reach another device: no remote copies, remote signals or barrier semaphores. Data moves between devices by JAX's collectives and lax.ppermute only.
A program may use at most 256 MiB of HBM per device.

v0:
```python
import jax
import jax.numpy as jnp
from jax import lax
from jax.sharding import PartitionSpec as P

HEAD = 64


def rms_norm(values, gain):
    return values * lax.rsqrt(jnp.mean(values * values, axis=-1, keepdims=True) + 1e-06) * gain


def rotate(values, cosine, sine):
    midpoint = values.shape[-1] // 2
    first_half = values[..., :midpoint]
    second_half = values[..., midpoint:]
    return jnp.concatenate(
        [first_half * cosine - second_half * sine, first_half * sine + second_half * cosine],
        axis=-1,
    )


def positions_of(segment):
    places = jnp.arange(segment.shape[0])
    matching = segment[:, None] == segment[None, :]
    earlier = places[None, :] < places[:, None]
    return jnp.sum(jnp.logical_and(matching, earlier).astype(jnp.int32), axis=1)


def angle_tables(segment):
    places = positions_of(segment).astype(jnp.float32)
    midpoint = HEAD // 2
    inverse = 10000.0 ** (-jnp.arange(midpoint).astype(jnp.float32) * 2.0 / HEAD)
    angles = places[:, None] * inverse[None, :]
    return (jnp.cos(angles)[:, None, :], jnp.sin(angles)[:, None, :])


def key_mask(segment):
    places = jnp.arange(segment.shape[0])
    matching = segment[:, None] == segment[None, :]
    allowed = matching & (segment[None, :] >= 0) & (places[None, :] <= places[:, None])
    return allowed | (places[None, :] == places[:, None])


def contract_rows(left, right):
    return lax.dot_general(
        left, right, (((0,), (0,)), ((), ())), preferred_element_type=jnp.float32
    )


def times_transpose(left, right):
    return lax.dot_general(
        left, right, (((1,), (1,)), ((), ())), preferred_element_type=jnp.float32
    )


def product(left, right):
    return jnp.dot(left, right, preferred_element_type=jnp.float32)


def column_sums(values):
    return jnp.sum(values.astype(jnp.float32), axis=0)


def masked_scores(query_rot, key_rot, allowed):
    scores = (
        jnp.einsum("qhd,khd->hqk", query_rot, key_rot, preferred_element_type=jnp.float32) * 0.125
    )
    return jnp.where(allowed[None], scores, -1e30)


def shards(
    activations,
    segment_ids,
    cotangent,
    querymat,
    keymat,
    valuemat,
    outmat,
    upmatrix,
    downmatrix,
    querybias,
    keybias,
    valuebias,
    outbias,
    upbias,
    downbias,
    firstgain,
    secondgain,
    thirdgain,
    fourthgain,
):
    gathered = (
        lax.all_gather(querymat, ("wide", "narrow"), axis=0, tiled=True),
        lax.all_gather(keymat, ("wide", "narrow"), axis=0, tiled=True),
        lax.all_gather(valuemat, ("wide", "narrow"), axis=0, tiled=True),
        lax.all_gather(outmat, ("wide", "narrow"), axis=0, tiled=True),
        lax.all_gather(upmatrix, ("wide", "narrow"), axis=0, tiled=True),
        lax.all_gather(downmatrix, ("wide", "narrow"), axis=0, tiled=True),
        lax.all_gather(querybias, ("wide", "narrow"), axis=0, tiled=True),
        lax.all_gather(keybias, ("wide", "narrow"), axis=0, tiled=True),
        lax.all_gather(valuebias, ("wide", "narrow"), axis=0, tiled=True),
        lax.all_gather(outbias, ("wide", "narrow"), axis=0, tiled=True),
        lax.all_gather(upbias, ("wide", "narrow"), axis=0, tiled=True),
        lax.all_gather(downbias, ("wide", "narrow"), axis=0, tiled=True),
        lax.all_gather(firstgain, ("wide", "narrow"), axis=0, tiled=True),
        lax.all_gather(secondgain, ("wide", "narrow"), axis=0, tiled=True),
        lax.all_gather(thirdgain, ("wide", "narrow"), axis=0, tiled=True),
        lax.all_gather(fourthgain, ("wide", "narrow"), axis=0, tiled=True),
    )
    (
        full_query,
        full_key,
        full_value,
        full_output,
        full_up,
        full_down,
        bias_query,
        bias_key,
        bias_value,
        bias_output,
        bias_up,
        bias_down,
        gain_first,
        gain_second,
        gain_third,
        gain_fourth,
    ) = gathered
    length = activations.shape[0]
    heads = full_query.shape[1] // HEAD
    width = full_query.shape[1]
    inputs = activations.astype(jnp.float32)
    cosine, sine = angle_tables(segment_ids)
    allowed = key_mask(segment_ids)
    valid_row = (segment_ids >= 0).astype(jnp.float32)
    normed_in, pull_first = jax.vjp(rms_norm, inputs, gain_first.astype(jnp.float32))
    normed_low = normed_in.astype(jnp.bfloat16)
    queries = product(normed_low, full_query) + bias_query.astype(jnp.float32)
    keys_pre = product(normed_low, full_key) + bias_key.astype(jnp.float32)
    values_pre = product(normed_low, full_value) + bias_value.astype(jnp.float32)
    query_rot = rotate(queries.reshape(length, heads, HEAD), cosine, sine).astype(jnp.bfloat16)
    key_rot = rotate(keys_pre.reshape(length, heads, HEAD), cosine, sine).astype(jnp.bfloat16)
    value_low = values_pre.reshape(length, heads, HEAD).astype(jnp.bfloat16)
    scores = masked_scores(query_rot, key_rot, allowed)
    peak = jnp.max(scores, axis=-1, keepdims=True)
    exponent = jnp.exp(scores - peak)
    totals = jnp.sum(exponent, axis=-1, keepdims=True)
    logsum = peak + jnp.log(totals)
    probs = exponent / totals
    mixed = jnp.einsum(
        "hqk,khd->qhd", probs.astype(jnp.bfloat16), value_low, preferred_element_type=jnp.float32
    )
    mixed_low = mixed.reshape(length, width).astype(jnp.bfloat16)
    attended = product(mixed_low, full_output) + bias_output.astype(jnp.float32)
    normed_att, pull_second = jax.vjp(rms_norm, attended, gain_second.astype(jnp.float32))
    middle = inputs + normed_att
    normed_mid, pull_third = jax.vjp(rms_norm, middle, gain_third.astype(jnp.float32))
    normed_mid_low = normed_mid.astype(jnp.bfloat16)
    expanded = product(normed_mid_low, full_up) + bias_up.astype(jnp.float32)
    activated_f, pull_gelu = jax.vjp(jax.nn.gelu, expanded)
    activated = activated_f.astype(jnp.bfloat16)
    contracted = product(activated, full_down) + bias_down.astype(jnp.float32)
    local_power = jnp.sum(valid_row * jnp.mean(contracted * contracted, axis=-1))
    power_total = lax.psum(local_power, ("wide", "narrow"))
    output_power = power_total / (length * lax.axis_size("wide") * lax.axis_size("narrow"))
    normed_out, pull_fourth = jax.vjp(rms_norm, contracted, gain_fourth.astype(jnp.float32))
    layer_out = (middle + normed_out).astype(jnp.bfloat16)
    again = (
        lax.all_gather(querymat, ("wide", "narrow"), axis=0, tiled=True),
        lax.all_gather(keymat, ("wide", "narrow"), axis=0, tiled=True),
        lax.all_gather(valuemat, ("wide", "narrow"), axis=0, tiled=True),
        lax.all_gather(outmat, ("wide", "narrow"), axis=0, tiled=True),
        lax.all_gather(upmatrix, ("wide", "narrow"), axis=0, tiled=True),
        lax.all_gather(downmatrix, ("wide", "narrow"), axis=0, tiled=True),
        lax.all_gather(querybias, ("wide", "narrow"), axis=0, tiled=True),
        lax.all_gather(keybias, ("wide", "narrow"), axis=0, tiled=True),
        lax.all_gather(valuebias, ("wide", "narrow"), axis=0, tiled=True),
        lax.all_gather(outbias, ("wide", "narrow"), axis=0, tiled=True),
        lax.all_gather(upbias, ("wide", "narrow"), axis=0, tiled=True),
        lax.all_gather(downbias, ("wide", "narrow"), axis=0, tiled=True),
        lax.all_gather(firstgain, ("wide", "narrow"), axis=0, tiled=True),
        lax.all_gather(secondgain, ("wide", "narrow"), axis=0, tiled=True),
        lax.all_gather(thirdgain, ("wide", "narrow"), axis=0, tiled=True),
        lax.all_gather(fourthgain, ("wide", "narrow"), axis=0, tiled=True),
    )
    back_query, back_key, back_value, back_output, back_up, back_down = (
        again[0],
        again[1],
        again[2],
        again[3],
        again[4],
        again[5],
    )
    seed = cotangent.astype(jnp.float32) * valid_row[:, None]
    d_contracted_f, fourth_slope = pull_fourth(seed)
    d_contracted = d_contracted_f.astype(jnp.bfloat16)
    down_slope = contract_rows(activated, d_contracted)
    down_bias_slope = column_sums(d_contracted)
    d_activated = times_transpose(d_contracted, back_down)
    d_expanded = pull_gelu(d_activated)[0].astype(jnp.bfloat16)
    up_slope = contract_rows(normed_mid_low, d_expanded)
    up_bias_slope = column_sums(d_expanded)
    d_normed_mid = times_transpose(d_expanded, back_up)
    d_middle_part, third_slope = pull_third(d_normed_mid)
    d_middle = seed + d_middle_part
    d_attended_f, second_slope = pull_second(d_middle)
    d_attended = d_attended_f.astype(jnp.bfloat16)
    output_slope = contract_rows(mixed_low, d_attended)
    output_bias_slope = column_sums(d_attended)
    d_mixed = (
        times_transpose(d_attended, back_output).astype(jnp.bfloat16).reshape(length, heads, HEAD)
    )
    probs_again = jnp.exp(masked_scores(query_rot, key_rot, allowed) - logsum)
    d_values = jnp.einsum(
        "hqk,qhd->khd",
        probs_again.astype(jnp.bfloat16),
        d_mixed,
        preferred_element_type=jnp.float32,
    )
    d_probs = jnp.einsum("qhd,khd->hqk", d_mixed, value_low, preferred_element_type=jnp.float32)
    row_terms = jnp.sum(probs_again * d_probs, axis=-1, keepdims=True)
    d_scores = (probs_again * (d_probs - row_terms)).astype(jnp.bfloat16)
    d_query_rot = (
        jnp.einsum("hqk,khd->qhd", d_scores, key_rot, preferred_element_type=jnp.float32) * 0.125
    )
    d_key_rot = (
        jnp.einsum("hqk,qhd->khd", d_scores, query_rot, preferred_element_type=jnp.float32) * 0.125
    )
    d_queries = rotate(d_query_rot, cosine, -sine).reshape(length, width).astype(jnp.bfloat16)
    d_keys = rotate(d_key_rot, cosine, -sine).reshape(length, width).astype(jnp.bfloat16)
    d_values_low = d_values.reshape(length, width).astype(jnp.bfloat16)
    query_slope = contract_rows(normed_low, d_queries)
    key_slope = contract_rows(normed_low, d_keys)
    value_slope = contract_rows(normed_low, d_values_low)
    query_bias_slope = column_sums(d_queries)
    key_bias_slope = column_sums(d_keys)
    value_bias_slope = column_sums(d_values_low)
    d_normed = (
        times_transpose(d_queries, back_query)
        + times_transpose(d_keys, back_key)
        + times_transpose(d_values_low, back_value)
    )
    d_inputs_part, first_slope = pull_first(d_normed)
    input_gradient = d_middle + d_inputs_part
    summed = (
        lax.psum_scatter(query_slope, ("wide", "narrow"), scatter_dimension=0, tiled=True),
        lax.psum_scatter(key_slope, ("wide", "narrow"), scatter_dimension=0, tiled=True),
        lax.psum_scatter(value_slope, ("wide", "narrow"), scatter_dimension=0, tiled=True),
        lax.psum_scatter(output_slope, ("wide", "narrow"), scatter_dimension=0, tiled=True),
        lax.psum_scatter(query_bias_slope, ("wide", "narrow"), scatter_dimension=0, tiled=True),
        lax.psum_scatter(key_bias_slope, ("wide", "narrow"), scatter_dimension=0, tiled=True),
        lax.psum_scatter(value_bias_slope, ("wide", "narrow"), scatter_dimension=0, tiled=True),
        lax.psum_scatter(output_bias_slope, ("wide", "narrow"), scatter_dimension=0, tiled=True),
        lax.psum_scatter(first_slope, ("wide", "narrow"), scatter_dimension=0, tiled=True),
        lax.psum_scatter(second_slope, ("wide", "narrow"), scatter_dimension=0, tiled=True),
        lax.psum_scatter(up_slope, ("wide", "narrow"), scatter_dimension=0, tiled=True),
        lax.psum_scatter(down_slope, ("wide", "narrow"), scatter_dimension=0, tiled=True),
        lax.psum_scatter(up_bias_slope, ("wide", "narrow"), scatter_dimension=0, tiled=True),
        lax.psum_scatter(down_bias_slope, ("wide", "narrow"), scatter_dimension=0, tiled=True),
        lax.psum_scatter(third_slope, ("wide", "narrow"), scatter_dimension=0, tiled=True),
        lax.psum_scatter(fourth_slope, ("wide", "narrow"), scatter_dimension=0, tiled=True),
    )
    attention_sums = summed[:10]
    feed_sums = summed[10:]
    return (
        layer_out,
        input_gradient,
        attention_sums[0],
        attention_sums[1],
        attention_sums[2],
        attention_sums[3],
        feed_sums[0],
        feed_sums[1],
        attention_sums[4],
        attention_sums[5],
        attention_sums[6],
        attention_sums[7],
        feed_sums[2],
        feed_sums[3],
        attention_sums[8],
        attention_sums[9],
        feed_sums[4],
        feed_sums[5],
        output_power,
    )


def solution(mesh):
    placed = (
        P(("wide", "narrow"), None),
        P(("wide", "narrow")),
        P(("wide", "narrow"), None),
        P(("wide", "narrow"), None),
        P(("wide", "narrow"), None),
        P(("wide", "narrow"), None),
        P(("wide", "narrow"), None),
        P(("wide", "narrow"), None),
        P(("wide", "narrow"), None),
        P(("wide", "narrow")),
        P(("wide", "narrow")),
        P(("wide", "narrow")),
        P(("wide", "narrow")),
        P(("wide", "narrow")),
        P(("wide", "narrow")),
        P(("wide", "narrow")),
        P(("wide", "narrow")),
        P(("wide", "narrow")),
        P(("wide", "narrow")),
    )
    return jax.shard_map(
        shards,
        mesh=mesh,
        in_specs=placed,
        out_specs=(
            P(("wide", "narrow"), None),
            P(("wide", "narrow"), None),
            P(("wide", "narrow"), None),
            P(("wide", "narrow"), None),
            P(("wide", "narrow"), None),
            P(("wide", "narrow"), None),
            P(("wide", "narrow"), None),
            P(("wide", "narrow"), None),
            P(("wide", "narrow")),
            P(("wide", "narrow")),
            P(("wide", "narrow")),
            P(("wide", "narrow")),
            P(("wide", "narrow")),
            P(("wide", "narrow")),
            P(("wide", "narrow")),
            P(("wide", "narrow")),
            P(("wide", "narrow")),
            P(("wide", "narrow")),
            P(),
        ),
        check_vma=False,
    )
```

profile of v0, /device:TPU:14, one launch (start us, length us, event | category | flops | bytes accessed | tf_op | source)
XLA Modules:
  0.0 1386.6 jit_solution(13215105580612590473)
XLA Ops:
  19.7 41.1 %all-reduce.20 = (bf16[1024]{0:T(1024)(128)(2,1)S(1)}, bf16[1024]{0:T(1024)(128)(2,1)S(1)}, bf16[1024]{0:T(1024)(128)(2,1)S(1)}, bf16[1024]{0:T(1024)(128)(2,1)S...) all-reduce(bf16[1024]{0:T(1024)(128)(2,1)S(1)} %dynamic-update-slic, ...), channel_id=1, replica_groups=mesh['wide'=16,'narrow'=2] {'wide','narrow'}, use_global_device_ids=true, to_apply=%add.1 | all-reduce | flops 9216 | bytes 36864
  62.6 28.8 %all-gather = bf16[32,1,128]{2,1,0:T(2,128)(2,1)S(1)} all-gather(bf16[1,1,128]{2,1,0:T(2,128)(2,1)} %bitcast.67), channel_id=1, replica_groups=mesh['wide'=16,'narrow'=2] {'wide','narrow'}, dimensions={0}, use_global_device_ids=true | all-gather | bytes 8448 | tf_op jit(solution)/shard_map/all_gather | solution.py:104
  100.8 24.7 %all-gather.10.cloned.1.call-done = bf16[1024,1024]{1,0:T(8,128)(2,1)} async-done(((bf16[32,1024]{1,0:T(8,128)(2,1)}), bf16[1024,1024]{1,0:T(8,128)(2,1)}) %all-gather.10.cloned.1.call-update) | async-done | bytes 2097168 | tf_op jit(solution)/shard_map/all_gather | solution.py:94
  131.7 52.0 %all-gather.12.cloned.1.call-done = bf16[1024,1024]{1,0:T(8,128)(2,1)} async-done(((bf16[32,1024]{1,0:T(8,128)(2,1)}), bf16[1024,1024]{1,0:T(8,128)(2,1)}) %all-gather.12.cloned.1.call-update) | async-done | bytes 2097168 | tf_op jit(solution)/shard_map/all_gather | solution.py:95
  200.4 8.4 fusion
  208.8 8.7 fusion.24
  217.5 24.1 %all-gather.14.cloned.1.call-done = bf16[1024,1024]{1,0:T(8,128)(2,1)} async-done(((bf16[32,1024]{1,0:T(8,128)(2,1)}), bf16[1024,1024]{1,0:T(8,128)(2,1)}) %all-gather.14.cloned.1.call-update) | async-done | bytes 2097168 | tf_op jit(solution)/shard_map/all_gather | solution.py:97
  246.8 74.6 %all-gather.16.cloned.1.call-done = bf16[1024,4096]{1,0:T(8,128)(2,1)} async-done(((bf16[32,4096]{1,0:T(8,128)(2,1)}), bf16[1024,4096]{1,0:T(8,128)(2,1)}) %all-gather.16.cloned.1.call-update) | async-done | bytes 8388624 | tf_op jit(solution)/shard_map/all_gather | solution.py:98
  321.4 11.8 fusion.38
  333.2 67.0 %all-gather.18.cloned.1.call-done = bf16[4096,1024]{1,0:T(8,128)(2,1)} async-done(((bf16[128,1024]{1,0:T(8,128)(2,1)}), bf16[4096,1024]{1,0:T(8,128)(2,1)}) %all-gather.18.cloned.1.call-update) | async-done | bytes 8388624 | tf_op jit(solution)/shard_map/all_gather | solution.py:99
  400.2 10.6 multiply_reduce_fusion.7
  415.5 17.0 %convert_reduce_fusion = (f32[4096]{0:T(1024)}, bf16[512,4096]{1,0:T(8,128)(2,1)}) fusion(f32[512,4096]{1,0:T(8,128)} %fusion.38, f32[4096]{0:T(1024)S(1)} %bitcast.65, bf16[512,1024]{1,0:T(8,128)(2,1)S(1)} %get-tuple-element.48, bf16[4096,1024]{1,0:T(8,128)(2,1)} %all-gather.18.cloned.1.call-done), kind=kOutput, calls=%fused_computation.18 | convolution fusion | flops 4343197696 | bytes 22052864 | tf_op jit(solution)/shard_map/dot_general | solution.py:52
  432.5 7.4 multiply_reduce_fusion.2
  454.7 9.0 convert_reduce_fusion.3
  467.3 9.0 multiply_reduce_fusion
  476.3 8.4 multiply_convert_fusion
  500.5 15.5 %fusion.48 = f32[4096,1024]{1,0:T(8,128)} fusion(bf16[512,1024]{1,0:T(8,128)(2,1)S(1)} %copy-done.23, f32[512,4096]{1,0:T(8,128)} %fusion.38, f32[4096]{0:T(1024)S(1)} %bitcast.66), kind=kOutput, calls=%fused_computation.114 | convolution fusion | flops 4315938816 | bytes 26230784 | tf_op jit(solution)/shard_map/dot_general | solution.py:46
  517.5 10.5 fusion.37
  537.4 41.4 %all-reduce.19 = (f32[1024]{0:T(1024)S(1)}, f32[1024]{0:T(1024)S(1)}, f32[1024]{0:T(1024)S(1)}, f32[1024]{0:T(1024)S(1)}, f32[4096]{0:T(1024)S(1)}, /*index=5*/f...) all-reduce(f32[1024]{0:T(1024)S(1)} %reduce_sum.252, ...), channel_id=8, replica_groups=mesh['wide'=16,'narrow'=2] {'wide','narrow'}, use_global_device_ids=true, to_apply=%region_19.20.clone | all-reduce | flops 13313 | bytes 106504
  588.7 107.0 %reduce-scatter.11.cloned.1.call-done = f32[32,1024]{1,0:T(8,128)} async-done(((f32[1024,1024]{1,0:T(8,128)}), f32[32,1024]{1,0:T(8,128)}) %reduce-scatter.11.cloned.1.call-update) | async-done | bytes 131088 | tf_op jit(solution)/shard_map/reduce_scatter | solution.py:248
  695.8 140.0 %reduce-scatter.9.cloned.1.call-done = f32[32,1024]{1,0:T(8,128)} async-done(((f32[1024,1024]{1,0:T(8,128)}), f32[32,1024]{1,0:T(8,128)}) %reduce-scatter.9.cloned.1.call-update) | async-done | bytes 131088 | tf_op jit(solution)/shard_map/reduce_scatter | solution.py:247
  835.8 139.0 %reduce-scatter.7.cloned.1.call-done = f32[32,1024]{1,0:T(8,128)} async-done(((f32[1024,1024]{1,0:T(8,128)}), f32[32,1024]{1,0:T(8,128)}) %reduce-scatter.7.cloned.1.call-update) | async-done | bytes 131088 | tf_op jit(solution)/shard_map/reduce_scatter | solution.py:246
  974.8 216.3 %reduce-scatter.17.cloned.1.call-done = f32[128,1024]{1,0:T(8,128)} async-done(((f32[4096,1024]{1,0:T(8,128)}), f32[128,1024]{1,0:T(8,128)}) %reduce-scatter.17.cloned.1.call-update) | async-done | bytes 524304 | tf_op jit(solution)/shard_map/reduce_scatter | solution.py:257
  1191.1 187.2 %reduce-scatter.15.cloned.1.call-done = f32[32,4096]{1,0:T(8,128)} async-done(((f32[1024,4096]{1,0:T(8,128)}), f32[32,4096]{1,0:T(8,128)}) %reduce-scatter.15.cloned.1.call-update) | async-done | bytes 524304 | tf_op jit(solution)/shard_map/reduce_scatter | solution.py:256
  (220 shorter events, 110.3 us)
Async XLA Ops:
  7.2 89.1 %copy-start.30 = (s32[512]{0:T(512)S(1)}, s32[512]{0:T(512)}, u32[]{:S(2)}) copy-start(s32[512]{0:T(512)} %param.20) | copy-start | bytes 6148
  7.2 89.4 %copy-start.4 = (bf16[512,1024]{1,0:T(8,128)(2,1)S(1)}, bf16[512,1024]{1,0:T(8,128)(2,1)}, u32[]{:S(2)}) copy-start(bf16[512,1024]{1,0:T(8,128)(2,1)} %param.19) | copy-start | bytes 3145732
  7.2 89.4 %all-gather.8.cloned.1.call-start = ((), (), s32[]{:S(2)}) async-start(), calls=%async_computation.6 | async-start | bytes 2162688 | tf_op jit(solution)/shard_map/all_gather | solution.py:96
  7.9 117.6 %all-gather.10.cloned.1.call-start = ((), (), s32[]{:S(2)}) async-start(), calls=%async_computation.7 | async-start | bytes 2162688 | tf_op jit(solution)/shard_map/all_gather | solution.py:94
  8.7 175.0 %all-gather.12.cloned.1.call-start = ((), (), s32[]{:S(2)}) async-start(), calls=%async_computation.8 | async-start | bytes 2162688 | tf_op jit(solution)/shard_map/all_gather | solution.py:95
  9.4 232.2 %all-gather.14.cloned.1.call-start = ((), (), s32[]{:S(2)}) async-start(), calls=%async_computation.9 | async-start | bytes 2162688 | tf_op jit(solution)/shard_map/all_gather | solution.py:97
  10.0 311.4 %all-gather.16.cloned.1.call-start = ((), (), s32[]{:S(2)}) async-start(), calls=%async_computation.10 | async-start | bytes 8650752 | tf_op jit(solution)/shard_map/all_gather | solution.py:98
  10.6 389.6 %all-gather.18.cloned.1.call-start = ((), (), s32[]{:S(2)}) async-start(), calls=%async_computation.11 | async-start | bytes 8650752 | tf_op jit(solution)/shard_map/all_gather | solution.py:99
  11.2 577.6 %reduce-scatter.13.cloned.1.call-start = ((), (), s32[]{:S(2)}) async-start(), calls=%async_computation.15 | async-start | bytes 4325376 | tf_op jit(solution)/shard_map/reduce_scatter | solution.py:249
  94.1 31.5 %copy-start.35 = (f32[512]{0:T(512)}, f32[512]{0:T(512)S(1)}, u32[]{:S(2)}) copy-start(f32[512]{0:T(512)S(1)} %fusion.31) | copy-start | bytes 6148
  244.9 76.5 %copy-start.37 = (f32[1024]{0:T(1024)S(1)}, f32[1024]{0:T(1024)}, u32[]{:S(2)}) copy-start(f32[1024]{0:T(1024)} %convert_element_type.170) | copy-start | bytes 12292
  246.8 193.1 %copy-start.46 = (f32[512]{0:T(512)}, f32[512]{0:T(512)S(1)}, u32[]{:S(2)}) copy-start(f32[512]{0:T(512)S(1)} %fusion.33) | copy-start | bytes 6148
  321.4 78.8 %copy-start.43 = (f32[32,1,128]{2,1,0:T(1,128)S(1)}, f32[32,1,128]{2,1,0:T(1,128)}, u32[]{:S(2)}) copy-start(f32[32,1,128]{2,1,0:T(1,128)} %convert_element_type.198) | copy-start | bytes 49156
  413.0 19.6 %slice-start = ((s8[8388608]{0:T(1024)(128)(4,1)}), s8[4194304]{0:T(1024)(128)(4,1)S(1)}, s32[]{:S(2)}) async-start(s8[8388608]{0:T(1024)(128)(4,1)} %bitcast.68), calls=%async_computation.18 | async-start | bytes 8388608
  415.5 17.0 %copy-start.22 = (bf16[512,1024]{1,0:T(8,128)(2,1)}, bf16[512,1024]{1,0:T(8,128)(2,1)S(1)}, u32[]{:S(2)}) copy-start(bf16[512,1024]{1,0:T(8,128)(2,1)S(1)} %get-tuple-element.48) | copy-start | bytes 3145732
  415.5 17.0 %slice-start.1 = ((s8[8388608]{0:T(1024)(128)(4,1)}), s8[4194304]{0:T(1024)(128)(4,1)S(1)}, s32[]{:S(2)}) async-start(s8[8388608]{0:T(1024)(128)(4,1)} %bitcast.68), calls=%async_computation.19 | async-start | bytes 8388608
  447.9 247.8 %reduce-scatter.11.cloned.1.call-start = ((), (), s32[]{:S(2)}) async-start(), calls=%async_computation.14 | async-start | bytes 4325376 | tf_op jit(solution)/shard_map/reduce_scatter | solution.py:248
  449.5 17.8 %copy-start.28 = (f32[16,512]{1,0:T(8,128)}, f32[16,512]{1,0:T(8,128)S(1)}, u32[]{:S(2)}) copy-start(f32[16,512]{1,0:T(8,128)S(1)} %log_add_fusion) | copy-start | bytes 98308
  467.2 368.6 %reduce-scatter.9.cloned.1.call-start = ((), (), s32[]{:S(2)}) async-start(), calls=%async_computation.13 | async-start | bytes 4325376 | tf_op jit(solution)/shard_map/reduce_scatter | solution.py:247
  495.6 479.2 %reduce-scatter.7.cloned.1.call-start = ((), (), s32[]{:S(2)}) async-start(), calls=%async_computation.12 | async-start | bytes 4325376 | tf_op jit(solution)/shard_map/reduce_scatter | solution.py:246
  499.3 691.8 %reduce-scatter.17.cloned.1.call-start = ((), (), s32[]{:S(2)}) async-start(), calls=%async_computation.17 | async-start | bytes 17301504 | tf_op jit(solution)/shard_map/reduce_scatter | solution.py:257
  516.0 862.4 %reduce-scatter.15.cloned.1.call-start = ((), (), s32[]{:S(2)}) async-start(), calls=%async_computation.16 | async-start | bytes 17301504 | tf_op jit(solution)/shard_map/reduce_scatter | solution.py:256
  534.3 51.0 %copy-start.34 = (f32[512]{0:T(512)S(1)}, f32[512]{0:T(512)}, u32[]{:S(2)}) copy-start(f32[512]{0:T(512)} %copy-done.33) | copy-start | bytes 6148
  534.3 51.0 %copy-start.1 = (f32[512,1024]{1,0:T(8,128)S(1)}, f32[512,1024]{1,0:T(8,128)}, u32[]{:S(2)}) copy-start(f32[512,1024]{1,0:T(8,128)} %copy-done) | copy-start | bytes 6291460
  (42 other events, 164.2 us)
Sparse Core Ops, SparseCore 0:
  10.9 56.0 all-gather.7
  69.9 55.6 all-gather.9
  128.4 55.2 all-gather.11
  186.4 55.2 all-gather.13
  244.3 77.0 all-gather.15
  324.1 76.0 all-gather.17
  448.1 107.9 reduce-scatter.12
  558.9 136.8 reduce-scatter.10
  698.6 137.1 reduce-scatter.8
  838.5 136.2 reduce-scatter.6
  977.6 213.4 reduce-scatter.16
  1193.8 184.4 reduce-scatter.14
where the time goes:
time: 1390 us
  waiting for transfers between devices  1040 us (75%)
  matrix products  151 us (11%)
  blocking collectives  111 us (8%)
  other arithmetic  40.9 us (3%)
  local copies, waits for them, and re-layouts  29.8 us (2%)
  between operations  16.9 us (1%)
    reduce_scatter x1, waiting for transfers between devices, shards(): lax.psum_scatter(down_slope, ('wide', 'narrow'), scatter_dimension=0, til...  216 us
    reduce_scatter x1, waiting for transfers between devices, shards(): lax.psum_scatter(up_slope, ('wide', 'narrow'), scatter_dimension=0, tiled...  187 us
    reduce_scatter x1, waiting for transfers between devices, shards(): lax.psum_scatter(key_slope, ('wide', 'narrow'), scatter_dimension=0, tile...  140 us
    reduce_scatter x1, waiting for transfers between devices, shards(): lax.psum_scatter(query_slope, ('wide', 'narrow'), scatter_dimension=0, ti...  139 us
    reduce_scatter x1, waiting for transfers between devices, shards(): lax.psum_scatter(value_slope, ('wide', 'narrow'), scatter_dimension=0, ti...  107 us
    unnamed x2, blocking collectives  82.4 us
    all_gather x1, waiting for transfers between devices, shards(): lax.all_gather(upmatrix, ('wide', 'narrow'), axis=0, tiled=True)  74.6 us
    all_gather x1, waiting for transfers between devices, shards(): lax.all_gather(downmatrix, ('wide', 'narrow'), axis=0, tiled=True)  67 us
  transfers between devices with their start and end apart: 12, of which 10 were waited for; matrix products, arithmetic and copies ran while one was open for 12% of the time, Pallas kernels for 0%

commit v1 on v0

--- a/solution.py
+++ b/solution.py
@@ -4,6 +4,18 @@
 from jax.sharding import PartitionSpec as P
 
 HEAD = 64
+
+
+def doubled_up(x, axis, dim):
+    ways, here = (lax.axis_size(axis), lax.axis_index(axis))
+    grown, reach = (x, 1)
+    while reach < ways:
+        theirs = lax.ppermute(grown, axis, [(d, d ^ reach) for d in range(ways)])
+        mine_first = jnp.concatenate([grown, theirs], axis=dim)
+        theirs_first = jnp.concatenate([theirs, grown], axis=dim)
+        grown = jnp.where(here & reach == 0, mine_first, theirs_first)
+        reach = 2 * reach
+    return grown
 
 
 def rms_norm(values, gain):
@@ -95,7 +107,7 @@
         lax.all_gather(keymat, ("wide", "narrow"), axis=0, tiled=True),
         lax.all_gather(valuemat, ("wide", "narrow"), axis=0, tiled=True),
         lax.all_gather(outmat, ("wide", "narrow"), axis=0, tiled=True),
-        lax.all_gather(upmatrix, ("wide", "narrow"), axis=0, tiled=True),
+        doubled_up(upmatrix, ("wide", "narrow"), 0),
         lax.all_gather(downmatrix, ("wide", "narrow"), axis=0, tiled=True),
         lax.all_gather(querybias, ("wide", "narrow"), axis=0, tiled=True),
         lax.all_gather(keybias, ("wide", "narrow"), axis=0, tiled=True),

time: 1390 us -> 1520 us (1.094)
  waiting for transfers between devices: 1040 us -> 1110 us
  blocking collectives: 111 us -> 142 us
    all_gather x1, waiting for transfers between devices: 24.1 us -> 172 us  [shards(): lax.all_gather(outmat, ('wide', 'narrow'), axis=0, tiled=True)]
    all_gather x1, waiting for transfers between devices: 52 us -> 0.02 us  [shards(): lax.all_gather(keymat, ('wide', 'narrow'), axis=0, tiled=True)]
    ppermute x0 -> x5, waiting for transfers between devices: none -> 40.2 us  [doubled_up(): theirs = lax.ppermute(grown, axis, [(d, d ^ reach) for d in range(ways)])]
    unnamed x2, blocking collectives: 82.4 us -> 114 us
    all_gather x1, waiting for transfers between devices: 74.6 us -> 46.2 us  [shards(): lax.all_gather(upmatrix, ('wide', 'narrow'), axis=0, tiled=True)]
    all_gather x1, waiting for transfers between devices: 24.7 us -> 0.01 us  [shards(): lax.all_gather(querymat, ('wide', 'narrow'), axis=0, tiled=True)]
  transfers between devices with their start and end apart: 12 -> 17, of which waited for: 10 -> 11; matrix products, arithmetic and copies ran while one was open for 12% -> 13% of each run, Pallas kernels for 0% -> 0%
where the time goes in v1:
time: 1520 us
  waiting for transfers between devices  1110 us (73%)
  matrix products  154 us (10%)
  blocking collectives  142 us (9%)
  other arithmetic  53.6 us (4%)
  local copies, waits for them, and re-layouts  23.9 us (2%)
  between operations  17.2 us (1%)
    reduce_scatter x1, waiting for transfers between devices, shards(): lax.psum_scatter(down_slope, ('wide', 'narrow'), scatter_dimension=0, til...  216 us
    reduce_scatter x1, waiting for transfers between devices, shards(): lax.psum_scatter(up_slope, ('wide', 'narrow'), scatter_dimension=0, tiled...  187 us
    all_gather x1, waiting for transfers between devices, shards(): lax.all_gather(outmat, ('wide', 'narrow'), axis=0, tiled=True)  172 us
    reduce_scatter x1, waiting for transfers between devices, shards(): lax.psum_scatter(key_slope, ('wide', 'narrow'), scatter_dimension=0, tile...  140 us
    reduce_scatter x1, waiting for transfers between devices, shards(): lax.psum_scatter(query_slope, ('wide', 'narrow'), scatter_dimension=0, ti...  140 us
    unnamed x2, blocking collectives  114 us
    reduce_scatter x1, waiting for transfers between devices, shards(): lax.psum_scatter(value_slope, ('wide', 'narrow'), scatter_dimension=0, ti...  106 us
    all_gather x1, waiting for transfers between devices, shards(): lax.all_gather(downmatrix, ('wide', 'narrow'), axis=0, tiled=True)  63.4 us
  transfers between devices with their start and end apart: 17, of which 11 were waited for; matrix products, arithmetic and copies ran while one was open for 13% of the time, Pallas kernels for 0%

profile of v1, /device:TPU:14, one launch (start us, length us, event | category | flops | bytes accessed | tf_op | source)
XLA Modules:
  0.0 1516.0 jit_solution(14649288851516226578)
XLA Ops:
  14.2 13.9 collective-permute-done.1
  29.4 24.5 %collective-permute-done.2 = bf16[128,4096]{1,0:T(8,128)(2,1)} collective-permute-done((bf16[128,4096]{1,0:T(8,128)(2,1)S(1)}, bf16[128,4096]{1,0:T(8,128)(2,1)}, u32[]{:S(2)}, u32[]{:S(2)}) %collective-permute-start.2) | collective-permute-done | bytes 1048608 | tf_op jit(solution)/shard_map/ppermute | solution.py:13
  59.8 72.6 %all-reduce.20 = (bf16[1024]{0:T(1024)(128)(2,1)S(1)}, bf16[1024]{0:T(1024)(128)(2,1)S(1)}, bf16[1024]{0:T(1024)(128)(2,1)S(1)}, bf16[1024]{0:T(1024)(128)(2,1)S...) all-reduce(bf16[1024]{0:T(1024)(128)(2,1)S(1)} %dynamic-update-slic, ...), channel_id=1, replica_groups=mesh['wide'=16,'narrow'=2] {'wide','narrow'}, use_global_device_ids=true, to_apply=%add.1 | all-reduce | flops 9216 | bytes 36864
  136.0 28.6 %all-gather = bf16[32,1,128]{2,1,0:T(2,128)(2,1)S(1)} all-gather(bf16[1,1,128]{2,1,0:T(2,128)(2,1)S(1)} %bitcast.66), channel_id=1, replica_groups=mesh['wide'=16,'narrow'=2] {'wide','narrow'}, dimensions={0}, use_global_device_ids=true | all-gather | bytes 8448 | tf_op jit(solution)/shard_map/all_gather | solution.py:116
  173.3 8.6 collective-permute-start.4
  217.4 8.6 fusion.31
  226.1 172.5 %all-gather.14.cloned.1.call-done = bf16[1024,1024]{1,0:T(8,128)(2,1)} async-done(((bf16[32,1024]{1,0:T(8,128)(2,1)}), bf16[1024,1024]{1,0:T(8,128)(2,1)}) %all-gather.14.cloned.1.call-update) | async-done | bytes 2097168 | tf_op jit(solution)/shard_map/all_gather | solution.py:109
  403.8 11.1 fusion.11
  414.9 63.4 %all-gather.16.cloned.1.call-done = bf16[4096,1024]{1,0:T(8,128)(2,1)} async-done(((bf16[128,1024]{1,0:T(8,128)(2,1)}), bf16[4096,1024]{1,0:T(8,128)(2,1)}) %all-gather.16.cloned.1.call-update) | async-done | bytes 8388624 | tf_op jit(solution)/shard_map/all_gather | solution.py:111
  478.3 10.6 multiply_reduce_fusion.7
  496.6 14.2 convert_reduce_fusion
  510.9 46.2 %all-gather.18.cloned.1.call-done = bf16[1024,4096]{1,0:T(8,128)(2,1)} async-done(((bf16[32,4096]{1,0:T(8,128)(2,1)}), bf16[1024,4096]{1,0:T(8,128)(2,1)}) %all-gather.18.cloned.1.call-update) | async-done | bytes 8388624 | tf_op jit(solution)/shard_map/all_gather | solution.py:185
  557.1 10.7 multiply_reduce_fusion.2
  583.6 9.0 convert_reduce_fusion.3
  596.2 9.0 multiply_reduce_fusion
  605.2 8.4 multiply_convert_fusion
  629.0 15.5 %fusion.55 = f32[4096,1024]{1,0:T(8,128)} fusion(bf16[512,1024]{1,0:T(8,128)(2,1)S(1)} %copy-done.23, f32[512,4096]{1,0:T(8,128)} %fusion.11, f32[4096]{0:T(1024)S(1)} %bitcast.65), kind=kOutput, calls=%fused_computation.126 | convolution fusion | flops 4315938816 | bytes 26230784 | tf_op jit(solution)/shard_map/dot_general | solution.py:58
  645.2 13.3 fusion.45
  667.8 41.3 %all-reduce.19 = (f32[1024]{0:T(1024)S(1)}, f32[1024]{0:T(1024)S(1)}, f32[1024]{0:T(1024)S(1)}, f32[1024]{0:T(1024)S(1)}, f32[4096]{0:T(1024)S(1)}, /*index=5*/f...) all-reduce(f32[1024]{0:T(1024)S(1)} %reduce_sum.252, ...), channel_id=8, replica_groups=mesh['wide'=16,'narrow'=2] {'wide','narrow'}, use_global_device_ids=true, to_apply=%region_19.20.clone | all-reduce | flops 13313 | bytes 106504
  719.1 105.7 %reduce-scatter.11.cloned.1.call-done = f32[32,1024]{1,0:T(8,128)} async-done(((f32[1024,1024]{1,0:T(8,128)}), f32[32,1024]{1,0:T(8,128)}) %reduce-scatter.11.cloned.1.call-update) | async-done | bytes 131088 | tf_op jit(solution)/shard_map/reduce_scatter | solution.py:260
  824.8 139.9 %reduce-scatter.9.cloned.1.call-done = f32[32,1024]{1,0:T(8,128)} async-done(((f32[1024,1024]{1,0:T(8,128)}), f32[32,1024]{1,0:T(8,128)}) %reduce-scatter.9.cloned.1.call-update) | async-done | bytes 131088 | tf_op jit(solution)/shard_map/reduce_scatter | solution.py:259
  964.6 139.6 %reduce-scatter.7.cloned.1.call-done = f32[32,1024]{1,0:T(8,128)} async-done(((f32[1024,1024]{1,0:T(8,128)}), f32[32,1024]{1,0:T(8,128)}) %reduce-scatter.7.cloned.1.call-update) | async-done | bytes 131088 | tf_op jit(solution)/shard_map/reduce_scatter | solution.py:258
  1104.2 216.2 %reduce-scatter.17.cloned.1.call-done = f32[128,1024]{1,0:T(8,128)} async-done(((f32[4096,1024]{1,0:T(8,128)}), f32[128,1024]{1,0:T(8,128)}) %reduce-scatter.17.cloned.1.call-update) | async-done | bytes 524304 | tf_op jit(solution)/shard_map/reduce_scatter | solution.py:269
  1320.4 187.2 %reduce-scatter.15.cloned.1.call-done = f32[32,4096]{1,0:T(8,128)} async-done(((f32[1024,4096]{1,0:T(8,128)}), f32[32,4096]{1,0:T(8,128)}) %reduce-scatter.15.cloned.1.call-update) | async-done | bytes 524304 | tf_op jit(solution)/shard_map/reduce_scatter | solution.py:268
  (251 shorter events, 128.4 us)
Async XLA Ops:
  7.2 174.7 %all-gather.8.cloned.1.call-start = ((), (), s32[]{:S(2)}) async-start(), calls=%async_computation.6 | async-start | bytes 2162688 | tf_op jit(solution)/shard_map/all_gather | solution.py:108
  7.9 178.2 %all-gather.10.cloned.1.call-start = ((), (), s32[]{:S(2)}) async-start(), calls=%async_computation.7 | async-start | bytes 2162688 | tf_op jit(solution)/shard_map/all_gather | solution.py:106
  8.7 183.7 %all-gather.12.cloned.1.call-start = ((), (), s32[]{:S(2)}) async-start(), calls=%async_computation.8 | async-start | bytes 2162688 | tf_op jit(solution)/shard_map/all_gather | solution.py:107
  9.4 389.1 %all-gather.14.cloned.1.call-start = ((), (), s32[]{:S(2)}) async-start(), calls=%async_computation.9 | async-start | bytes 2162688 | tf_op jit(solution)/shard_map/all_gather | solution.py:109
  10.0 468.3 %all-gather.16.cloned.1.call-start = ((), (), s32[]{:S(2)}) async-start(), calls=%async_computation.10 | async-start | bytes 8650752 | tf_op jit(solution)/shard_map/all_gather | solution.py:111
  10.6 546.5 %all-gather.18.cloned.1.call-start = ((), (), s32[]{:S(2)}) async-start(), calls=%async_computation.11 | async-start | bytes 8650752 | tf_op jit(solution)/shard_map/all_gather | solution.py:185
  10.6 1.8 collective-permute-start
  13.6 14.5 collective-permute-start.1
  28.3 25.6 %collective-permute-start.2 = (bf16[128,4096]{1,0:T(8,128)(2,1)S(1)}, bf16[128,4096]{1,0:T(8,128)(2,1)}, u32[]{:S(2)}, u32[]{:S(2)}) collective-permute-start(bf16[128,4096]{1,0:T(8,128)(2,1)S(1)} %maximum_select_fusion.4), channel_id=1, source_target_pairs={{0,4},{1,5},{2,6},{3,7},{4,0},{5,1},{6,2},{7,3},{8,12},{9,13},{10,... | collective-permute-start | bytes 3145736 | tf_op jit(solution)/shard_map/ppermute | solution.py:13
  29.4 106.6 %copy-start.51 = (bf16[128]{0:T(256)(128)(2,1)S(1)}, bf16[128]{0:T(256)(128)(2,1)}, u32[]{:S(2)}) copy-start(bf16[128]{0:T(256)(128)(2,1)} %param.32) | copy-start | bytes 772
  29.4 135.8 %copy-start.2 = (bf16[512,1024]{1,0:T(8,128)(2,1)S(1)}, bf16[512,1024]{1,0:T(8,128)(2,1)}, u32[]{:S(2)}) copy-start(bf16[512,1024]{1,0:T(8,128)(2,1)} %param.19) | copy-start | bytes 3145732
  57.0 110.9 %collective-permute-start.3 = (bf16[256,4096]{1,0:T(8,128)(2,1)S(1)}, bf16[256,4096]{1,0:T(8,128)(2,1)}, u32[]{:S(2)}, u32[]{:S(2)}) collective-permute-start(bf16[256,4096]{1,0:T(8,128)(2,1)S(1)} %maximum_select_fusion.3), channel_id=1, source_target_pairs={{0,8},{1,9},{2,10},{3,11},{4,12},{5,13},{6,14},{7,15},{8,0},{9,1},... | collective-permute-start | bytes 6291464 | tf_op jit(solution)/shard_map/ppermute | solution.py:13
  57.4 661.6 %reduce-scatter.13.cloned.1.call-start = ((), (), s32[]{:S(2)}) async-start(), calls=%async_computation.15 | async-start | bytes 4325376 | tf_op jit(solution)/shard_map/reduce_scatter | solution.py:261
  173.3 230.4 %collective-permute-start.4 = (bf16[512,4096]{1,0:T(8,128)(2,1)}, bf16[512,4096]{1,0:T(8,128)(2,1)}, u32[]{:S(2)}, u32[]{:S(2)}) collective-permute-start(bf16[512,4096]{1,0:T(8,128)(2,1)} %maximum_select_fusion.2), channel_id=1, source_target_pairs={{0,16},{1,17},{2,18},{3,19},{4,20},{5,21},{6,22},{7,23},{8,24},{9,... | collective-permute-start | bytes 12582920 | tf_op jit(solution)/shard_map/ppermute | solution.py:13
  403.7 164.0 %copy-start.45 = (f32[512]{0:T(512)}, f32[512]{0:T(512)S(1)}, u32[]{:S(2)}) copy-start(f32[512]{0:T(512)S(1)} %fusion.40) | copy-start | bytes 6148
  403.7 74.5 %copy-start.29 = (f32[1024]{0:T(1024)S(1)}, f32[1024]{0:T(1024)}, u32[]{:S(2)}) copy-start(f32[1024]{0:T(1024)} %convert_element_type.174) | copy-start | bytes 12292
  403.8 74.5 %copy-start.42 = (f32[32,1,128]{2,1,0:T(1,128)S(1)}, f32[32,1,128]{2,1,0:T(1,128)}, u32[]{:S(2)}) copy-start(f32[32,1,128]{2,1,0:T(1,128)} %convert_element_type.198) | copy-start | bytes 49156
  577.0 247.8 %reduce-scatter.11.cloned.1.call-start = ((), (), s32[]{:S(2)}) async-start(), calls=%async_computation.14 | async-start | bytes 4325376 | tf_op jit(solution)/shard_map/reduce_scatter | solution.py:260
  596.1 368.5 %reduce-scatter.9.cloned.1.call-start = ((), (), s32[]{:S(2)}) async-start(), calls=%async_computation.13 | async-start | bytes 4325376 | tf_op jit(solution)/shard_map/reduce_scatter | solution.py:259
  624.3 479.9 %reduce-scatter.7.cloned.1.call-start = ((), (), s32[]{:S(2)}) async-start(), calls=%async_computation.12 | async-start | bytes 4325376 | tf_op jit(solution)/shard_map/reduce_scatter | solution.py:258
  627.8 692.6 %reduce-scatter.17.cloned.1.call-start = ((), (), s32[]{:S(2)}) async-start(), calls=%async_computation.17 | async-start | bytes 17301504 | tf_op jit(solution)/shard_map/reduce_scatter | solution.py:269
  644.5 863.2 %reduce-scatter.15.cloned.1.call-start = ((), (), s32[]{:S(2)}) async-start(), calls=%async_computation.16 | async-start | bytes 17301504 | tf_op jit(solution)/shard_map/reduce_scatter | solution.py:268
  664.7 50.9 %copy-start.33 = (f32[512]{0:T(512)S(1)}, f32[512]{0:T(512)}, u32[]{:S(2)}) copy-start(f32[512]{0:T(512)} %copy-done.32) | copy-start | bytes 6148
  664.7 50.9 %copy-start.1 = (f32[512,1024]{1,0:T(8,128)S(1)}, f32[512,1024]{1,0:T(8,128)}, u32[]{:S(2)}) copy-start(f32[512,1024]{1,0:T(8,128)} %copy-done) | copy-start | bytes 6291460
  (56 other events, 501.6 us)
Sparse Core Ops, SparseCore 0:
  10.9 57.7 all-gather.7
  71.5 55.3 all-gather.9
  129.7 55.4 all-gather.11
  187.9 210.5 all-gather.13
  401.2 77.0 all-gather.15
  481.0 76.0 all-gather.17
  577.1 107.6 reduce-scatter.12
  687.7 137.0 reduce-scatter.10
  827.6 136.9 reduce-scatter.8
  967.3 136.8 reduce-scatter.6
  1107.1 213.2 reduce-scatter.16
  1323.2 184.4 reduce-scatter.14
